TPU v7x, 512 devices: a whole 4x8x8 slice. The times are simulated.
512 devices in a mesh: replica: 64 (over y, z), tensor: 8 (over x, core).
Axes of the slice: x: 4, y: 8, z: 8, core: 2. Of those that a mesh axis runs over, the one named last changes fastest.
Arguments:
- hidden: bfloat16 [2048, 1536], P(('replica', 'tensor')), may hold values from -6 to 6
- attn_gain: float32 [1536], replicated, may hold values from 0.25 to 1.75
- w_query: bfloat16 [1536, 1536], P(None, 'tensor'), may hold values from -0.625 to 0.625
- w_keyvalue: bfloat16 [1536, 8, 128], P(None, 'tensor'), may hold values from -0.4375 to 0.4375
- w_output: bfloat16 [1536, 1536], P('tensor'), may hold values from -0.625 to 0.625
- cache: bfloat16 [4608, 128, 8, 128], P('replica', None, 'tensor')
- page_table: int32 [2048, 16], P('replica'), may hold values from -1 to 199, as said below
- ctx_len: int32 [2048], P('replica'), may hold values from 1 to 2048, as said below
- move_dest: int32 [2048], P('replica'), may hold values from 0 to 63, as said below
- ffn_gain: float32 [1536], replicated, may hold values from 0.25 to 1.75
- router: bfloat16 [1536, 40], replicated, may hold values from -0.15625 to 0.15625
- routes: int32 [2048, 8], P('replica'), may hold values from 0 to 39, all different within a row
- w_in: bfloat16 [1536, 2, 1024], P(None, None, 'tensor'), may hold values from -0.15625 to 0.15625
- w_down: bfloat16 [1024, 1536], P('tensor'), may hold values from -0.25 to 0.25
Outputs:
- attended: bfloat16 [2048, 1536], P(('replica', 'tensor'))
- experts_out: bfloat16 [2048, 1536], P(('replica', 'tensor'))
Inputs may be any that keep to these rules, and one draw needn't show every extreme that they name: `move_dest`: replica r's 32 entries name where its pool rows 40 to 71 go, in order: 16 other replicas, 2 pages each, never r itself; one replica drawn from the seed receives pages from every other. `page_table`: row i holds request i's pages in order and -1 after its last page; each request has one page or more; every lent page is used by exactly one request of the replica it goes to, and no pool page twice. `ctx_len`: with n pages in its row, a request holds between (n - 1) * 128 + 1 and n * 128 cached tokens. `routes`: each row names 8 different experts.
All inputs are finite; a program needn't handle non-finite values.
Results may differ from a plain program's by a relative error of at most 0.02.
Values may be sent and summed in bfloat16 or wider, within the bound.
A program may use at most 64 MiB of HBM per device.

v0:
```python
import math

import jax
import jax.numpy as jnp
from jax import lax
from jax.sharding import PartitionSpec as P

HEAD_DIM = 64
EXPERTS = 40
FF = 512
CAP = 2


ATTN_SCALE = 0.015625
RESID_SCALE = 0.22
ROPE_BASE = 10000.0
EPSILON = 1e-06
NEG_FILL = -1e30


def rms_norm(row_block, gain):
    values = row_block.astype(jnp.float32)
    factor = lax.rsqrt(jnp.mean(values * values, axis=-1, keepdims=True) + EPSILON)
    return (values * factor * gain).astype(jnp.bfloat16)


def rotate(values, positions):
    lanes = values.shape[-1]
    halfway = lanes // 2
    indices = jnp.arange(halfway, dtype=jnp.float32)
    inverse = jnp.exp(indices * (-2.0 * math.log(ROPE_BASE) / lanes))
    angles = positions.astype(jnp.float32)[:, None] * inverse[None, :]
    cosine = jnp.concatenate([jnp.cos(angles), jnp.cos(angles)], axis=-1)[:, None, :]
    sine_rep = jnp.concatenate([jnp.sin(angles), jnp.sin(angles)], axis=-1)[:, None, :]
    turned = jnp.concatenate([-values[..., halfway:], values[..., :halfway]], axis=-1)
    return values * cosine + turned * sine_rep


def page_partials(queries, page_rows, spans):
    head_dim = queries.shape[-1]
    scores = (
        jnp.einsum(
            "pkgh,ptkh->pkgt",
            queries,
            page_rows[..., :head_dim],
            preferred_element_type=jnp.float32,
        )
        * ATTN_SCALE
    )
    in_range = (jnp.arange(page_rows.shape[1], dtype=jnp.int32)[None, :] < spans[:, None])[
        :, None, None, :
    ]
    scores = jnp.where(in_range, scores, NEG_FILL)
    part_max = jnp.max(scores, axis=-1)
    weights = jnp.where(in_range, jnp.exp(scores - part_max[..., None]), 0.0)
    part_sum = jnp.sum(weights, axis=-1)
    part_out = jnp.einsum(
        "pkgt,ptkh->pkgh",
        weights.astype(jnp.bfloat16),
        page_rows[..., head_dim:],
        preferred_element_type=jnp.float32,
    )
    return (part_max, part_sum, part_out)


def claimed_by(entries, owners, spans, slot_count):
    matches = entries[None, :] == jnp.arange(slot_count, dtype=jnp.int32)[:, None]
    holders = jnp.sum(jnp.where(matches, owners[None, :] + 1, 0), axis=1) - 1
    held_spans = jnp.sum(jnp.where(matches, spans[None, :], 0), axis=1)
    return (holders, held_spans)


def on_device(
    hidden,
    attn_gain,
    w_query,
    w_keyvalue,
    w_output,
    cache,
    page_table,
    ctx_len,
    move_dest,
    ffn_gain,
    router,
    routes,
    w_in,
    w_down,
):
    replicas = lax.axis_size("replica")
    tensor_id = lax.axis_index("tensor")
    pool = cache.shape[0]
    outgoing = move_dest.shape[0]
    local_pages = pool - outgoing
    page_len = cache.shape[1]
    kv_local = cache.shape[2]
    requests = page_table.shape[0]
    groups = w_query.shape[1] // (kv_local * HEAD_DIM)
    inbox = replicas * CAP
    hidden_all = lax.all_gather(hidden, "tensor", axis=0, tiled=True)
    normed = rms_norm(hidden_all, attn_gain)
    queries = jnp.dot(normed, w_query, preferred_element_type=jnp.float32).reshape(
        requests, kv_local * groups, HEAD_DIM
    )
    queries = (
        rotate(queries, ctx_len).astype(jnp.bfloat16).reshape(requests, kv_local, groups, HEAD_DIM)
    )
    projected = jnp.dot(
        normed,
        w_keyvalue.reshape(w_keyvalue.shape[0], kv_local * 2 * HEAD_DIM),
        preferred_element_type=jnp.float32,
    ).reshape(requests, kv_local, 2 * HEAD_DIM)
    new_key = rotate(projected[..., :HEAD_DIM], ctx_len).astype(jnp.bfloat16)
    new_value = projected[..., HEAD_DIM:].astype(jnp.bfloat16)
    entries = page_table.reshape(-1)
    positions = jnp.arange(entries.shape[0], dtype=jnp.int32)
    owners = positions // page_table.shape[1]
    slot_idx = positions % page_table.shape[1]
    spans = jnp.where(entries >= 0, jnp.clip(ctx_len[owners] - slot_idx * page_len, 0, page_len), 0)
    out_slots = jnp.arange(outgoing, dtype=jnp.int32)
    earlier = (move_dest[None, :] == move_dest[:, None]) & (out_slots[None, :] < out_slots[:, None])
    send_slot = move_dest * CAP + jnp.sum(earlier, axis=1)
    slot_match = send_slot[None, :] == jnp.arange(inbox, dtype=jnp.int32)[:, None]
    send_page = local_pages + jnp.sum(jnp.where(slot_match, out_slots[None, :], 0), axis=1)
    outbound = jnp.take(cache, send_page, axis=0)
    inbound = lax.all_to_all(
        outbound.reshape(replicas, CAP, page_len, kv_local, 2 * HEAD_DIM),
        "replica",
        split_axis=0,
        concat_axis=0,
        tiled=True,
    )
    page_rows = jnp.concatenate(
        [cache, inbound.reshape(inbox, page_len, kv_local, 2 * HEAD_DIM)], axis=0
    )
    holders, held_spans = claimed_by(entries, owners, spans, pool + inbox)
    part_max, part_sum, part_out = page_partials(
        queries[jnp.maximum(holders, 0)], page_rows, held_spans
    )
    slots_total = part_max.shape[0]
    new_score = (
        jnp.einsum("rkgh,rkh->rkg", queries, new_key, preferred_element_type=jnp.float32)
        * ATTN_SCALE
    )
    member = holders[None, :] == jnp.arange(requests, dtype=jnp.int32)[:, None]
    highest = jnp.maximum(
        new_score, jnp.max(jnp.where(member[:, :, None, None], part_max[None], NEG_FILL), axis=1)
    )
    rescale = jnp.where(
        (holders >= 0)[:, None, None], jnp.exp(part_max - highest[jnp.maximum(holders, 0)]), 0.0
    )
    fresh_weight = jnp.exp(new_score - highest)
    indicator = member.astype(jnp.float32)
    denominator = (
        jnp.dot(
            indicator,
            (rescale * part_sum).reshape(slots_total, -1),
            precision=lax.Precision.HIGHEST,
        ).reshape(requests, kv_local, groups)
        + fresh_weight
    )
    numerator = jnp.dot(
        indicator,
        (rescale[..., None] * part_out).reshape(slots_total, -1),
        precision=lax.Precision.HIGHEST,
    ).reshape(requests, kv_local, groups, HEAD_DIM)
    numerator = numerator + fresh_weight[..., None] * new_value.astype(jnp.float32)[:, :, None, :]
    attention = (
        (numerator / denominator[..., None])
        .astype(jnp.bfloat16)
        .reshape(requests, kv_local * groups * HEAD_DIM)
    )
    row_block = attention
    summed = lax.psum_scatter(
        jnp.dot(row_block, w_output, preferred_element_type=jnp.float32),
        "tensor",
        scatter_dimension=0,
        tiled=True,
    )
    attended = (hidden.astype(jnp.float32) + RESID_SCALE * summed).astype(jnp.bfloat16)
    ffn_input = lax.all_gather(rms_norm(attended, ffn_gain), "tensor", axis=0, tiled=True)
    units = w_down.shape[0]
    unit_expert = (tensor_id * units + jnp.arange(units, dtype=jnp.int32)) // FF
    expert_ids = jnp.arange(EXPERTS, dtype=jnp.int32)
    row_block = ffn_input
    logits = jnp.dot(row_block, router, preferred_element_type=jnp.float32)
    picked = jnp.sum(
        jnp.where(routes[:, :, None] == expert_ids[None, None, :], logits[:, None, :], 0.0), axis=2
    )
    gate_weights = jax.nn.softmax(picked, axis=-1)
    spread = jnp.sum(
        jnp.where(routes[:, :, None] == unit_expert[None, None, :], gate_weights[:, :, None], 0.0),
        axis=1,
    )
    lifted = jnp.einsum("rd,dsu->rsu", row_block, w_in, preferred_element_type=jnp.float32)
    active = (jax.nn.silu(lifted[:, 0]) * lifted[:, 1] * spread).astype(jnp.bfloat16)
    experts_out = lax.psum_scatter(
        jnp.dot(active, w_down, preferred_element_type=jnp.float32),
        "tensor",
        scatter_dimension=0,
        tiled=True,
    ).astype(jnp.bfloat16)
    return (attended, experts_out)


def solution(mesh):
    placed = (
        P(("replica", "tensor"), None),
        P(),
        P(None, "tensor"),
        P(None, "tensor", None),
        P("tensor", None),
        P("replica", None, "tensor", None),
        P("replica", None),
        P("replica"),
        P("replica"),
        P(),
        P(),
        P("replica", None),
        P(None, None, "tensor"),
        P("tensor", None),
    )
    return jax.shard_map(
        on_device,
        mesh=mesh,
        in_specs=placed,
        out_specs=(P(("replica", "tensor"), None), P(("replica", "tensor"), None)),
        check_vma=False,
    )
```

profile of v0, /device:TPU:1, one launch (start us, length us, event | category | flops | bytes accessed | tf_op | source)
XLA Modules:
  0.0 315.0 jit_solution(6150158538750811166)
XLA Ops:
  8.9 4.7 %gather_fusion.1 = bf16[128,128,128]{2,1,0:T(8,128)(2,1)} fusion(bf16[72,128,128]{2,1,0:T(8,128)(2,1)} %bitcast.125, s32[1024]{0:T(1024)S(1)} %pad_clamp_fusion), kind=kCustom, calls=%fused_computation.1 | custom fusion | bytes 8389120 | tf_op jit(solution)/shard_map/jit(_take)/gather | solution.py:124
  13.6 6.4 %copy.54 = bf16[128,128,128]{1,2,0:T(8,128)(2,1)} copy(bf16[128,128,128]{2,1,0:T(8,128)(2,1)} %gather_fusion.1) | data formatting | bytes 8388608 | tf_op jit(solution)/shard_map/jit(_take)/gather | solution.py:124
  20.3 4.6 %broadcast_select_fusion = bf16[64,2,128,1,128]{2,4,1,3,0:T(8,128)(2,1)} fusion(bf16[64,2,128,1,128]{2,4,1,3,0:T(8,128)(2,1)} %bitcast.126, pred[64,2]{1,0:T(8,128)(4,1)S(1)} %compare_and_fusion), kind=kLoop, calls=%fused_computation.5 | loop fusion | flops 2097152 | bytes 8388736 | tf_op jit(solution)/shard_map/jit(_take)/select_n | solution.py:124
  24.9 17.5 %all-to-all-start = ((bf16[64,2,128,1,128]{2,4,1,3,0:T(8,128)(2,1)}), bf16[64,2,128,1,128]{2,4,1,3,0:T(8,128)(2,1)}, u32[]{:S(2)}, u32[]{:S(2)}) async-start(bf16[64,2,128,1,128]{2,4,1,3,0:T(8,128)(2,1)} %broadcast_select_fusion), calls=%async_computation | async-start | bytes 8388608 | tf_op jit(solution)/shard_map/all_to_all | solution.py:125
  42.6 2.5 copy.55
  45.1 14.0 %all-gather = bf16[8,4,1536]{2,1,0:T(4,128)(2,1)S(1)} all-gather(bf16[1,4,1536]{2,1,0:T(4,128)(2,1)S(1)} %bitcast.127), channel_id=1, replica_groups=mesh['replica'=64,'tensor'=8] {'tensor'}, dimensions={0}, use_global_device_ids=true | all-gather | bytes 110592 | tf_op jit(solution)/shard_map/all_gather | solution.py:99
  59.2 1.4 fusion.82
  61.2 1.2 convolution_bitcast_fusion
  63.1 1.4 copy.61
  66.0 4.4 %compare_select_fusion.2 = s32[512,1]{0,1:T(1,128)S(1)} fusion(s32[]{:T(128)} %bitcast.26, s32[]{:T(128)} %bitcast.27, s32[]{:T(128)} %bitcast.28, s32[]{:T(128)} %bitcast.29, s32[]{:T(128)} %bitcast.30, s32[]{:T(128)} %bitcast.32, s32[]{:T(128)} %bitcast.31), kind=kLoop, calls=%fused_computation.120 | loop fusion | flops 11776 | bytes 2076 | tf_op jit(solution)/shard_map/gather | solution.py:118
  71.2 15.6 %fusion.70 = s32[512]{0:T(512)S(1)} fusion(pred[512]{0:T(512)(128)(4,1)S(1)} %compare_reduce_fusion, pred[512]{0:T(512)(128)(4,1)S(1)} %compare_reduce_fusion.1, pred[512]{0:T(512)(128)(4,1)S(1)} %compare_reduce_fusion.2, pred[512]{0:T(512)(128)(4,1)S(1)} %compare_reduce_fusion.3, pred[512]{0:T(512)(128)(4,1)S(1)} %compare_reduce_fusion.4, ...), kind=kLoop, calls=%fused_computation.149 | loop fusion | flops 18432 | bytes 19044 | tf_op jit(solution)/shard_map/jit(_where)/select_n | solution.py:118
  87.1 1.6 gather_fusion
  88.7 1.3 dynamic-slice
  91.4 68.1 %all-to-all-done = bf16[64,2,128,1,128]{2,4,1,3,0:T(8,128)(2,1)} async-done(((bf16[64,2,128,1,128]{2,4,1,3,0:T(8,128)(2,1)}), bf16[64,2,128,1,128]{2,4,1,3,0:T(8,128)(2,1)}, u32[]{:S(2)}, u32[]{:S(2)}) %all-to-all-start) | async-done | bytes 4194336 | tf_op jit(solution)/shard_map/all_to_all | solution.py:125
  159.5 3.5 %fusion.86 = (f32[200,3]{1,0:T(8,128)S(1)}, f32[200,3,128]{2,1,0:T(4,128)}) fusion(bf16[200,3,64]{2,1,0:T(4,128)(2,1)} %gather_fusion, bf16[72,128,1,128]{1,3,0,2:T(8,128)(2,1)S(1)} %copy-done.2, bf16[128,128,1,128]{1,3,0,2:T(8,128)(2,1)} %bitcast.43, pred[200,128]{1,0:T(8,128)(4,1)S(1)} %iota_compare_fusion.2), kind=kOutput, calls=%fused_computation.180 | convolution fusion | flops 11698600 | bytes 6965600 | tf_op jit(solution)/shard_map/pkgh,ptkh->pkgt/dot_general | solution.py:42
  164.6 2.2 fusion.22
  167.5 3.7 %fusion.11 = f32[200,3,64]{2,1,0:T(4,128)S(1)} fusion(bf16[128,128,1,128]{1,3,0,2:T(8,128)(2,1)} %bitcast.43, bf16[72,128,1,128]{1,3,0,2:T(8,128)(2,1)S(1)} %copy-done.2, f32[200,3,128]{2,1,0:T(4,128)} %get-tuple-element.54, f32[200,3]{1,0:T(8,128)} %copy-done.3, f32[200,3]{1,0:T(8,128)S(1)} %exponential_select_fusion.1, pred[200,128]{1,0:T(8,128)(4,1)} %copy-done.7), kind=kOutput, calls=%fused_computation.14 | convolution fusion | flops 16652800 | bytes 7044800 | tf_op jit(solution)/shard_map/pkgt,ptkh->pkgh/dot_general | solution.py:57
  171.3 1.2 convolution_add_fusion.1
  172.5 1.0 fusion.15
  173.6 2.0 fusion.87
  175.6 89.5 %all-reduce.5.cloned.1.call-done = f32[32,1536]{1,0:T(8,128)} async-done(((f32[32,1536]{1,0:T(8,128)}), f32[32,1536]{1,0:T(8,128)}) %all-reduce.5.cloned.1.call-update) | async-done | bytes 196624
  266.9 14.6 %all-gather.1 = bf16[8,4,1536]{2,1,0:T(4,128)(2,1)S(1)} all-gather(bf16[1,4,1536]{2,1,0:T(4,128)(2,1)S(1)} %fusion.52), channel_id=1, replica_groups=mesh['replica'=64,'tensor'=8] {'tensor'}, dimensions={0}, use_global_device_ids=true | all-gather | bytes 110592 | tf_op jit(solution)/shard_map/all_gather | solution.py:180
  281.6 1.0 fusion.88
  285.1 22.4 %all-reduce.6 = bf16[32,1536]{1,0:T(8,128)(2,1)S(1)} all-reduce(f32[32,1536]{1,0:T(8,128)S(1)} %fusion.55), channel_id=3, replica_groups=mesh['replica'=64,'tensor'=8] {'tensor'}, use_global_device_ids=true, to_apply=%region_14.15.clone | all-reduce | flops 49152 | bytes 294912
  (116 shorter events, 14.3 us)
Async XLA Ops:
  7.2 277.5 %copy-start = (bf16[1536,2,128]{2,1,0:T(2,128)(2,1)S(1)}, bf16[1536,2,128]{2,1,0:T(2,128)(2,1)}, u32[]{:S(2)}) copy-start(bf16[1536,2,128]{2,1,0:T(2,128)(2,1)} %param.26) | copy-start | bytes 2359300
  24.9 17.6 %copy-start.1 = (bf16[72,128,1,128]{3,1,2,0:T(8,128)(2,1)S(1)}, bf16[72,128,1,128]{3,1,2,0:T(8,128)(2,1)}, u32[]{:S(2)}) copy-start(bf16[72,128,1,128]{3,1,2,0:T(8,128)(2,1)} %param.19) | copy-start | bytes 7077892
  24.9 134.6 %all-to-all-start = ((bf16[64,2,128,1,128]{2,4,1,3,0:T(8,128)(2,1)}), bf16[64,2,128,1,128]{2,4,1,3,0:T(8,128)(2,1)}, u32[]{:S(2)}, u32[]{:S(2)}) async-start(bf16[64,2,128,1,128]{2,4,1,3,0:T(8,128)(2,1)} %broadcast_select_fusion), calls=%async_computation | async-start | bytes 8388608 | tf_op jit(solution)/shard_map/all_to_all | solution.py:125
  42.4 2.6 copy-start.8
  42.5 16.7 %copy-start.10 = (f32[1536]{0:T(1024)S(1)}, f32[1536]{0:T(1024)}, u32[]{:S(2)}) copy-start(f32[1536]{0:T(1024)} %param.15) | copy-start | bytes 18436
  42.5 18.3 %copy-start.5 = (s32[32]{0:T(128)S(1)}, s32[32]{0:T(128)}, u32[]{:S(2)}) copy-start(s32[32]{0:T(128)} %param.21) | copy-start | bytes 388
  42.5 18.3 %copy-start.12 = (s32[32,16]{0,1:T(8,128)S(1)}, s32[32,16]{0,1:T(8,128)}, u32[]{:S(2)}) copy-start(s32[32,16]{0,1:T(8,128)} %param.20) | copy-start | bytes 6148
  42.5 222.7 %all-reduce.5.cloned.1.call-start = ((), (), s32[]{:S(2)}) async-start(), calls=%async_computation.1 | async-start | bytes 393216
  45.1 114.5 %copy-start.2 = (bf16[72,128,1,128]{1,3,0,2:T(8,128)(2,1)S(1)}, bf16[72,128,1,128]{1,3,0,2:T(8,128)(2,1)}, u32[]{:S(2)}) copy-start(bf16[72,128,1,128]{1,3,0,2:T(8,128)(2,1)} %copy.55) | copy-start | bytes 7077892
  59.2 1.9 copy-start.13
  87.0 76.0 %copy-start.11 = (s32[200]{0:T(256)}, s32[200]{0:T(256)S(1)}, u32[]{:S(2)}) copy-start(s32[200]{0:T(256)S(1)} %get-tuple-element.17) | copy-start | bytes 2404
  90.7 73.8 %copy-start.7 = (pred[200,128]{1,0:T(8,128)(4,1)}, pred[200,128]{1,0:T(8,128)(4,1)S(1)}, u32[]{:S(2)}) copy-start(pred[200,128]{1,0:T(8,128)(4,1)S(1)} %iota_compare_fusion.2) | copy-start | bytes 76804
  163.0 3.7 %copy-start.3 = (f32[200,3]{1,0:T(8,128)}, f32[200,3]{1,0:T(8,128)S(1)}, u32[]{:S(2)}) copy-start(f32[200,3]{1,0:T(8,128)S(1)} %get-tuple-element.53) | copy-start | bytes 7204
  166.9 0.6 copy-start.4
  171.2 113.8 %copy-start.6 = (bf16[128,1536]{1,0:T(8,128)(2,1)S(1)}, bf16[128,1536]{1,0:T(8,128)(2,1)}, u32[]{:S(2)}) copy-start(bf16[128,1536]{1,0:T(8,128)(2,1)} %param.27) | copy-start | bytes 1179652
  266.1 42.0 %copy-start.9 = (bf16[4,1536]{1,0:T(4,128)(2,1)}, bf16[4,1536]{1,0:T(4,128)(2,1)S(1)}, u32[]{:S(2)}) copy-start(bf16[4,1536]{1,0:T(4,128)(2,1)S(1)} %get-tuple-element.5) | copy-start | bytes 36868
Sparse Core Ops, SparseCore 0:
  175.7 89.3 all-reduce.4
where the time goes:
time: 318 us; the launch traced here: 315 us
  waiting for transfers between devices  158 us (50%)
  blocking collectives  51 us (16%)
  other arithmetic  35.5 us (11%)
  local copies, waits for them, and re-layouts  22.6 us (7%)
  starting transfers between devices  17.6 us (6%)
  matrix products  15.5 us (5%)
  between operations  15.1 us (5%)
    unnamed x2, waiting for transfers between devices  89.5 us
    all_to_all x1, waiting for transfers between devices, on_device(): lax.all_to_all(outbound.reshape(replicas, CAP, page_len, kv_local, 2 * HE...  68.1 us
    unnamed x1, blocking collectives  22.4 us
    all_to_all x1, starting transfers between devices, on_device(): lax.all_to_all(outbound.reshape(replicas, CAP, page_len, kv_local, 2 * HE...  17.5 us
    select_n x1, other arithmetic, on_device(): jnp.where(entries >= 0, jnp.clip(ctx_len[owners] - slot_idx * page_len, 0...  15.6 us
    all_gather x1, blocking collectives, on_device(): lax.all_gather(rms_norm(attended, ffn_gain), 'tensor', axis=0, tiled=True)  14.6 us
    all_gather x1, blocking collectives, on_device(): hidden_all = lax.all_gather(hidden, 'tensor', axis=0, tiled=True)  14 us
    gather x2, local copies, waits for them, and re-layouts, on_device(): outbound = jnp.take(cache, send_page, axis=0)  11.1 us
  transfers between devices with their start and end apart: 2, of which 2 were waited for; matrix products, arithmetic and copies ran while one was open for 11% of the time, Pallas kernels for 0%

commit v1 on v0

v1 whole, which is shorter than its diff:
```python
import functools
import math

import jax
import jax.numpy as jnp
from jax import lax
from jax.experimental import pallas as pl
from jax.experimental.pallas import tpu as pltpu
from jax.sharding import PartitionSpec as P

HEAD_DIM = 64
EXPERTS = 40
FF = 512
CAP = 2
PAGE = 128
GROUPS = 3
ROWS = 8

ATTN_SCALE = 0.015625
RESID_SCALE = 0.22
ROPE_BASE = 10000.0
EPSILON = 1e-06
NEG_FILL = -1e30

BF = jnp.bfloat16
F32 = jnp.float32
I32 = jnp.int32
MESH = pl.DeviceIdType.MESH


def iota(shape, axis):
    return lax.broadcasted_iota(I32, shape, axis)


def mm(a, b):
    return lax.dot_general(a, b, (((1,), (0,)), ((), ())), preferred_element_type=F32)


def mm_t(a, b):
    return lax.dot_general(a, b, (((1,), (1,)), ((), ())), preferred_element_type=F32)


def roll4(v):
    return pltpu.roll(v, 4, 0)


def unfold(p0, p1, tensors):
    low = iota((8, p0.shape[1]), 0) < 4
    parts = []
    for a in range(tensors // 2):
        lo = p0[16 * a : 16 * a + 8] + roll4(p1[16 * a : 16 * a + 8])
        hi = roll4(p0[16 * a + 8 : 16 * a + 16]) + p1[16 * a + 8 : 16 * a + 16]
        parts.append(jnp.where(low, lo, hi))
    return jnp.concatenate(parts, axis=0)


def expand(v, tensors):
    low = iota((8, v.shape[1]), 0) < 4
    first, second = [], []
    for a in range(tensors // 2):
        piece = v[8 * a : 8 * a + 8]
        turned = roll4(piece)
        first.append(jnp.where(low, piece, 0.0))
        second.append(jnp.where(low, 0.0, turned))
        first.append(jnp.where(low, turned, 0.0))
        second.append(jnp.where(low, 0.0, piece))
    return jnp.concatenate(first, axis=0).astype(BF), jnp.concatenate(second, axis=0).astype(BF)


def page_rows(q_rows, pages):
    count = pages.shape[0]
    lane = iota((count * 8, 128), 1)
    span = jnp.where(lane < 64, pltpu.roll(q_rows, 64, 1), q_rows)
    query = jnp.where(lane < 64, q_rows, 0.0).reshape(count, 8, 128).astype(BF)
    scores = lax.dot_general(
        query, pages, (((2,), (2,)), ((0,), (0,))), preferred_element_type=F32
    ).reshape(count * 8, 128) * ATTN_SCALE
    in_range = lane.astype(F32) < span
    scores = jnp.where(in_range, scores, NEG_FILL)
    top = jnp.max(scores, axis=1, keepdims=True)
    weights = jnp.where(in_range, jnp.exp(scores - top), 0.0)
    total = jnp.sum(weights, axis=1, keepdims=True)
    out = lax.dot_general(
        weights.reshape(count, 8, 128).astype(BF),
        pages,
        (((2,), (1,)), ((0,), (0,))),
        preferred_element_type=F32,
    ).reshape(count * 8, 128)
    coarse = top.astype(BF).astype(F32)
    rows = jnp.where(
        lane < 16, coarse, jnp.where(lane < 32, top - coarse, jnp.where(lane < 64, total, out))
    )
    return rows.astype(BF)


def kernel(
    R, T, B, NL, LOCAL, POOL, OUT, UNITS,
    hid, again, wq, wkv, wo, cache, ptab, ctx, mdest, fgain, router, routes, win, wdown,
    att_o, exp_o,
    hid_v, again_v, wq_v, wkv_v, wo_v, cache_v, ptab_v, ctx_v, mdest_v, fgain_v, router_v,
    routes_v, win_v, wdown_v, win_f, wgu_v, fold_v, a1_v, qg_v, loc_v, att_v, exp_v,
    xg, msg, inq, ret_s, ret, rs_s, rs, fg, es_s, es,
    isem, osem, ready, ssem, rsem,
):
    r = lax.axis_index("replica")
    t = lax.axis_index("tensor")
    D = hid.shape[1]
    H = D // 2
    NZ = math.isqrt(R)
    y, z = r // NZ, lax.rem(r, NZ)
    NIN = R * ROWS
    NR = GROUPS * B

    loads = []

    def load(src, dst):
        copy = pltpu.make_async_copy(src, dst, isem.at[len(loads)])
        copy.start()
        loads.append(copy)
        return copy

    get_hid = load(hid, hid_v)
    get_again = load(again, again_v)
    get_ptab = load(ptab, ptab_v)
    get_ctx = load(ctx, ctx_v)
    get_mdest = load(mdest, mdest_v)
    get_wq = load(wq, wq_v.at[0 : GROUPS * HEAD_DIM])
    get_wkv = load(wkv, wkv_v)
    get_cache = load(cache, cache_v)
    get_win = load(win, win_v)
    get_wo = load(wo, wo_v.at[0 : GROUPS * HEAD_DIM])
    get_wdown = load(wdown, wdown_v)
    get_router = load(router, router_v.at[0:EXPERTS])
    get_routes = load(routes, routes_v)
    get_fgain = load(fgain, fgain_v)

    barrier = pltpu.get_barrier_semaphore()
    for k in range(1, T):
        pl.semaphore_signal(barrier, inc=1, device_id=(r, lax.rem(t + k, T)), device_id_type=MESH)
    for k in range(1, NZ):
        pl.semaphore_signal(
            barrier, inc=1, device_id=(lax.rem(y + k, NZ) * NZ + z, t), device_id_type=MESH
        )
        pl.semaphore_signal(
            barrier, inc=1, device_id=(y * NZ + lax.rem(z + k, NZ), t), device_id_type=MESH
        )

    low8 = iota((8, H), 0) < 4

    def normalise(folded, gain):
        squares = jnp.sum(folded * folded, axis=1, keepdims=True)
        mean = (squares + roll4(jnp.broadcast_to(squares, (8, 128)))[:, 0:1]) * (1.0 / D)
        return folded * lax.rsqrt(mean + EPSILON) * gain

    def fold_gain(ref):
        left = jnp.broadcast_to(ref[:, 0:H], (8, H))
        right = jnp.broadcast_to(ref[:, H:D], (8, H))
        return jnp.where(low8, left, right)

    get_hid.wait()
    get_again.wait()
    hidden = hid_v[...].astype(F32)
    fold_v[0:4, :] = hidden[:, 0:H]
    fold_v[4:8, :] = hidden[:, H:D]
    xg[t] = normalise(fold_v[...], fold_gain(again_v)).astype(BF)

    pl.semaphore_wait(barrier, (T - 1) + 2 * (NZ - 1))
    for k in range(1, NZ):
        pl.semaphore_signal(
            ready, inc=1, device_id=(y * NZ + lax.rem(z + k, NZ), t), device_id_type=MESH
        )

    def share(buf, phase):
        for k in range(1, T):
            pltpu.make_async_remote_copy(
                buf.at[t], buf.at[t], ssem.at[phase], rsem.at[phase],
                device_id=(r, lax.rem(t + k, T)), device_id_type=MESH,
            ).start()

    def scatter(src, dst, phase):
        for k in range(1, T):
            peer = lax.rem(t + k, T)
            pltpu.make_async_remote_copy(
                src.at[peer], dst.at[t], ssem.at[phase], rsem.at[phase],
                device_id=(r, peer), device_id_type=MESH,
            ).start()

    def exchange(src, dst, phase):
        def step(k, carry):
            peer = lax.rem(r + k, R)
            pltpu.make_async_remote_copy(
                src.at[peer], dst.at[r], ssem.at[phase], rsem.at[phase],
                device_id=(peer, t), device_id_type=MESH,
            ).start()
            return carry

        lax.fori_loop(1, R, step, 0)

    def arrived(buf, sems, phase):
        part = buf.at[0 : buf.shape[0] - 1]
        pltpu.make_async_copy(part, part, sems.at[phase]).wait()

    share(xg, 0)

    get_ptab.wait()
    get_ctx.wait()
    get_mdest.wait()
    table = ptab_v[...]
    slots = table.shape[0]
    ctx_row = ctx_v[...]
    spans = jnp.where(
        table >= 0, jnp.clip(ctx_row - iota((slots, B), 0) * PAGE, 0, PAGE), 0
    )
    tile = (iota((B, 4 * B), 0) == (iota((B, 4 * B), 1) & (B - 1))).astype(F32).astype(BF)
    table_w = mm(table.astype(F32).astype(BF), tile)
    spans_w = mm(spans.astype(F32).astype(BF), tile)
    CH = 64 if NL % 64 == 0 and NIN % 64 == 0 else 32

    def claims(base, page, head):
        found = jnp.zeros((CH, 4 * B), F32)
        pages = page.astype(F32)
        for k in range(slots):
            found = found + jnp.where(pages == table_w[k : k + 1, :], spans_w[k : k + 1, :], 0.0)
        group = iota((CH, 4 * B), 1) // B
        flag = jnp.where((group == head) & (found > 0.0), 1.0, 0.0)
        rows = jnp.where(group == GROUPS, found, flag)
        a1_v[pl.ds(base, CH), :] = jnp.where(head < GROUPS, rows, 0.0).astype(BF)

    def local_claims(c, carry):
        row = iota((CH, 4 * B), 0) + c * CH
        page = jnp.where(row < LOCAL * 8, row >> 3, -2)
        claims(pl.multiple_of(c * CH, CH), page, row & 7)
        return carry

    def inbox_claims(c, carry):
        row = iota((CH, 4 * B), 0) + c * CH
        claims(pl.multiple_of(NL + c * CH, CH), POOL + (row >> 2), row & 3)
        return carry

    lax.fori_loop(0, NL // CH, local_claims, 0)
    lax.fori_loop(0, NIN // CH, inbox_claims, 0)

    dest_row = mdest_v[...]
    dest_sq = jnp.broadcast_to(dest_row, (OUT, OUT))
    sub_sq, lane_sq = iota((OUT, OUT), 0), iota((OUT, OUT), 1)
    dest_col = jnp.sum(jnp.where(sub_sq == lane_sq, dest_sq, 0).astype(F32), axis=1, keepdims=True)
    dest_f = dest_sq.astype(F32)
    earlier = (dest_col == dest_f) & (sub_sq < lane_sq)
    rank = jnp.sum(jnp.where(earlier, 1.0, 0.0), axis=0, keepdims=True)
    slot_row = dest_f * CAP + rank
    slot_sq = slot_row[0:8, :]
    NQ = OUT * 8
    grow = (iota((OUT, NQ), 0) == (iota((OUT, NQ), 1) >> 3)).astype(F32).astype(BF)
    slot_lane = mm(slot_sq.astype(BF), grow)[0:1, :]
    pick = iota((NQ, OUT), 1) == (iota((NQ, OUT), 0) >> 3)
    slot_sub = jnp.sum(
        jnp.where(pick, jnp.broadcast_to(slot_row[0:1, :], (NQ, OUT)), 0.0), axis=1, keepdims=True
    )

    def fetch_map():
        row, lane = iota((NQ, NIN), 0), iota((NQ, NIN), 1)
        same = (lane >> 2).astype(F32) == slot_sub
        hit = same & ((row & 7) == (lane & 3)) & ((lane & 3) < GROUPS)
        return jnp.where(hit, 1.0, 0.0).astype(BF)

    def place_map():
        row, lane = iota((NIN, NQ), 0), iota((NIN, NQ), 1)
        same = (row >> 2).astype(F32) == slot_lane
        hit = same & ((lane & 7) == (row & 3)) & ((row & 3) < GROUPS)
        return jnp.where(hit, 1.0, 0.0).astype(BF)

    sq_b = iota((B, B), 0) == iota((B, B), 1)
    ctx_col = jnp.sum(
        jnp.where(sq_b, jnp.broadcast_to(ctx_row, (B, B)), 0).astype(F32), axis=1, keepdims=True
    )
    lane_b = iota((B, 128), 1)
    freq = (lane_b & 31).astype(F32)
    angle = ctx_col * jnp.exp(freq * (-2.0 * math.log(ROPE_BASE) / HEAD_DIM))
    cosine = jnp.cos(angle)
    sine = jnp.sin(angle)
    front = (lane_b & 63) < 32
    sine = jnp.where(front, -sine, sine)

    def rotate(v):
        turned = jnp.where(front, pltpu.roll(v, 96, 1), pltpu.roll(v, 32, 1))
        return (v * cosine + turned * sine).astype(BF).astype(F32)

    inq[r] = jnp.zeros((ROWS, 128), BF)
    ret[r] = jnp.zeros((ROWS, 128), BF)
    wq_v[GROUPS * HEAD_DIM :, :] = jnp.zeros((HEAD_DIM, D), BF)
    wo_v[GROUPS * HEAD_DIM :, :] = jnp.zeros((HEAD_DIM, D), BF)
    router_v[EXPERTS:, :] = jnp.zeros((128 - EXPERTS, D), BF)
    get_wq.wait()
    get_wkv.wait()

    arrived(xg, rsem, 0)
    normed = xg[...].astype(F32).reshape(T * 8, H).astype(BF)
    q_all = [mm_t(normed, wq_v[:, c * H : (c + 1) * H]) for c in range(2)]
    kv_all = [mm(normed, wkv_v[c * H : (c + 1) * H, :]) for c in range(2)]
    q01 = rotate(unfold(q_all[0][:, 0:128], q_all[1][:, 0:128], T))
    q2 = rotate(unfold(q_all[0][:, 128:256], q_all[1][:, 128:256], T))
    new_kv = unfold(kv_all[0], kv_all[1], T)
    head_lane = lane_b < 64
    heads = [
        jnp.where(head_lane, q01, 0.0),
        jnp.where(head_lane, pltpu.roll(q01, 64, 1), 0.0),
        jnp.where(head_lane, q2, 0.0),
    ]
    marker = jnp.where(head_lane, 0.0, 1.0)
    qg_v[...] = jnp.concatenate(heads + [marker], axis=0).astype(BF)

    msg[...] = mm(a1_v[NL:, :], qg_v[...]).reshape(R, ROWS, 128).astype(BF)
    pl.semaphore_wait(ready, NZ - 1)
    exchange(msg, inq, 1)

    get_cache.wait()
    loc_v[0 : LOCAL * 8, :] = page_rows(
        mm(a1_v[0 : LOCAL * 8, :], qg_v[...]), cache_v[0:LOCAL]
    )
    if NL > LOCAL * 8:
        loc_v[LOCAL * 8 :, :] = jnp.zeros((NL - LOCAL * 8, 128), BF)
    eye = (iota((4 * B, 4 * B), 0) == iota((4 * B, 4 * B), 1)).astype(F32).astype(BF)
    owned_loc = mm_t(eye, a1_v[0:NL, :])[0:NR] > 0.5
    owned_in = mm_t(eye, a1_v[NL:, :])[0:NR] > 0.5
    lane_sel = iota((NR, 128), 1)
    max_sel = jnp.where((lane_sel == 0) | (lane_sel == 16), 1.0, 0.0).astype(BF)
    new_key = rotate(new_kv)
    new_score = jnp.concatenate(
        [jnp.sum(h * new_key, axis=1, keepdims=True) for h in heads], axis=0
    ) * ATTN_SCALE
    fresh = jnp.where(head_lane, 1.0, new_kv.astype(BF).astype(F32))
    fresh = jnp.concatenate([fresh] * GROUPS, axis=0)
    loc = loc_v[...]
    score_loc = jnp.where(owned_loc, mm_t(max_sel, loc), NEG_FILL)
    top_loc = jnp.maximum(new_score, jnp.max(score_loc, axis=1, keepdims=True))
    sum_loc = mm(jnp.exp(score_loc - top_loc).astype(BF), loc)
    sum_loc = sum_loc + jnp.exp(new_score - top_loc) * fresh
    fetch = fetch_map()
    place = place_map()

    arrived(inq, rsem, 1)
    sent = inq[...].astype(F32).reshape(NIN, 128).astype(BF)
    lent = page_rows(mm(fetch, sent), cache_v[LOCAL:POOL])
    ret_s[...] = mm(place, lent).reshape(R, ROWS, 128).astype(BF)
    exchange(ret_s, ret, 2)

    get_win.wait()
    win_f[...] = win_v[...].astype(F32)
    wgu_v[:, 0:UNITS] = win_f[pl.ds(0, D, stride=2), :].astype(BF)
    wgu_v[:, UNITS:] = win_f[pl.ds(1, D, stride=2), :].astype(BF)
    get_wo.wait()
    get_wdown.wait()
    get_router.wait()
    get_routes.wait()
    get_fgain.wait()
    eye_b = sq_b.astype(F32).astype(BF)
    chosen = mm_t(eye_b, routes_v[...].astype(F32).astype(BF))
    expert = iota((B, 128), 1)
    expert_f = expert.astype(F32)
    picked = jnp.zeros((B, 128), F32)
    for k in range(routes.shape[0]):
        picked = jnp.where(expert_f == chosen[:, k : k + 1], 1.0, picked)
    mine = expert == (t * UNITS) // FF
    gain_f = fold_gain(fgain_v)
    residual = fold_v[...]

    arrived(ret, rsem, 2)
    back = ret[...].astype(F32).reshape(NIN, 128).astype(BF)
    score_in = jnp.where(owned_in, mm_t(max_sel, back), NEG_FILL)
    top = jnp.maximum(top_loc, jnp.max(score_in, axis=1, keepdims=True))
    merged = jnp.exp(top_loc - top) * sum_loc + mm(jnp.exp(score_in - top).astype(BF), back)
    attention = (merged / merged[:, 32:33]).astype(BF).astype(F32)
    att0, att1, att2 = (attention[g * B : (g + 1) * B] for g in range(GROUPS))
    left = jnp.where(head_lane, pltpu.roll(att0, 64, 1), att1)
    right = jnp.where(head_lane, pltpu.roll(att2, 64, 1), 0.0)
    left1, left2 = expand(left, T)
    right1, right2 = expand(right, T)
    rows1 = jnp.concatenate([left1, right1], axis=1)
    rows2 = jnp.concatenate([left2, right2], axis=1)
    partial = mm(rows1, wo_v[:, 0:H]) + mm(rows2, wo_v[:, H:D])
    partial = partial.reshape(T, 8, H).astype(BF)
    rs_s[...] = partial
    scatter(rs_s, rs, 3)
    rs[t] = rs_s[t]
    arrived(rs, rsem, 3)
    summed = jnp.sum(rs[...].astype(F32), axis=0)
    attended = (residual + RESID_SCALE * summed).astype(BF)
    attended_f = attended.astype(F32)
    fg[t] = normalise(attended_f, gain_f).astype(BF)
    share(fg, 4)
    att_v[:, 0:H] = attended_f[0:4].astype(BF)
    att_v[:, H:D] = attended_f[4:8].astype(BF)
    put_att = pltpu.make_async_copy(att_v, att_o, osem.at[0])
    put_att.start()

    arrived(fg, rsem, 4)
    ffn = fg[...].astype(F32).reshape(T * 8, H).astype(BF)
    up_all = [mm(ffn, wgu_v[c * H : (c + 1) * H, :]) for c in range(2)]
    log_all = [mm_t(ffn, router_v[:, c * H : (c + 1) * H]) for c in range(2)]
    gate = unfold(up_all[0][:, 0:UNITS], up_all[1][:, 0:UNITS], T)
    up = unfold(up_all[0][:, UNITS:], up_all[1][:, UNITS:], T)
    logits = jnp.where(picked > 0.0, unfold(log_all[0], log_all[1], T), NEG_FILL)
    chances = jnp.exp(logits - jnp.max(logits, axis=1, keepdims=True))
    chances = jnp.where(picked > 0.0, chances, 0.0)
    share_of = jnp.sum(jnp.where(mine, chances, 0.0), axis=1, keepdims=True) / jnp.sum(
        chances, axis=1, keepdims=True
    )
    active = gate * (1.0 / (1.0 + jnp.exp(-gate))) * up * share_of
    act1, act2 = expand(active, T)
    down = mm(act1, wdown_v[:, 0:H]) + mm(act2, wdown_v[:, H:D])
    es_s[...] = down.reshape(T, 8, H).astype(BF)
    scatter(es_s, es, 5)
    es[t] = es_s[t]
    arrived(es, rsem, 5)
    experts = jnp.sum(es[...].astype(F32), axis=0)
    exp_v[:, 0:H] = experts[0:4].astype(BF)
    exp_v[:, H:D] = experts[4:8].astype(BF)
    put_exp = pltpu.make_async_copy(exp_v, exp_o, osem.at[1])
    put_exp.start()
    for phase, buf in enumerate((xg, inq, ret, rs, fg, es)):
        arrived(buf, ssem, phase)
    put_att.wait()
    put_exp.wait()


def on_device(
    hidden,
    attn_gain,
    w_query,
    w_keyvalue,
    w_output,
    cache,
    page_table,
    ctx_len,
    move_dest,
    ffn_gain,
    router,
    routes,
    w_in,
    w_down,
):
    R = lax.axis_size("replica")
    T = lax.axis_size("tensor")
    D = hidden.shape[1]
    H = D // 2
    B = page_table.shape[0]
    POOL = cache.shape[0]
    OUT = move_dest.shape[0]
    LOCAL = POOL - OUT
    UNITS = w_down.shape[0]
    NL = -(-LOCAL * 8 // 128) * 128
    NIN = R * ROWS
    args = (
        hidden,
        attn_gain.reshape(1, D),
        w_query.T,
        w_keyvalue.reshape(D, 2 * HEAD_DIM),
        w_output,
        cache.reshape(POOL, PAGE, 2 * HEAD_DIM),
        page_table.T,
        ctx_len.reshape(1, B),
        move_dest.reshape(1, OUT),
        ffn_gain.reshape(1, D),
        router.T,
        routes.T,
        w_in.reshape(2 * D, UNITS),
        w_down,
    )
    vm = pltpu.VMEM
    landing = [vm(a.shape, a.dtype) for a in args]
    landing[2] = vm((256, D), BF)
    landing[4] = vm((256, D), BF)
    landing[10] = vm((128, D), BF)
    any_spec = pl.BlockSpec(memory_space=pl.ANY)
    group = vm((T, 8, H), BF)
    inbox = vm((R, ROWS, 128), BF)
    scratch = landing + [
        vm((2 * D, UNITS), F32),
        vm((D, 2 * UNITS), BF),
        vm((8, H), F32),
        vm((NL + NIN, 4 * B), BF),
        vm((4 * B, 128), BF),
        vm((NL, 128), BF),
        vm((4, D), BF),
        vm((4, D), BF),
        group,
        inbox,
        inbox,
        inbox,
        inbox,
        group,
        group,
        group,
        group,
        group,
        pltpu.SemaphoreType.DMA((len(args),)),
        pltpu.SemaphoreType.DMA((2,)),
        pltpu.SemaphoreType.REGULAR,
        pltpu.SemaphoreType.DMA((6,)),
        pltpu.SemaphoreType.DMA((6,)),
    ]
    shape = jax.ShapeDtypeStruct((4, D), BF)
    return pl.pallas_call(
        functools.partial(kernel, R, T, B, NL, LOCAL, POOL, OUT, UNITS),
        out_shape=(shape, shape),
        in_specs=[any_spec] * len(args),
        out_specs=(any_spec, any_spec),
        scratch_shapes=scratch,
        name="decode_step",
        compiler_params=pltpu.CompilerParams(
            collective_id=0, has_side_effects=True, vmem_limit_bytes=32 * 1024 * 1024
        ),
    )(*args)


def solution(mesh):
    placed = (
        P(("replica", "tensor"), None),
        P(),
        P(None, "tensor"),
        P(None, "tensor", None),
        P("tensor", None),
        P("replica", None, "tensor", None),
        P("replica", None),
        P("replica"),
        P("replica"),
        P(),
        P(),
        P("replica", None),
        P(None, None, "tensor"),
        P("tensor", None),
    )
    return jax.shard_map(
        on_device,
        mesh=mesh,
        in_specs=placed,
        out_specs=(P(("replica", "tensor"), None), P(("replica", "tensor"), None)),
        check_vma=False,
    )
```

time: 318 us -> 66.9 us (0.21)
  waiting for transfers between devices: 158 us -> 0 us
  Pallas kernels: 0 us -> 51.8 us
  blocking collectives: 51 us -> 0 us
  other arithmetic: 35.5 us -> 0 us
  starting transfers between devices: 17.6 us -> 0 us
  matrix products: 15.5 us -> 0 us
  between operations: 15.1 us -> 0.65 us
  local copies, waits for them, and re-layouts: 22.6 us -> 13.8 us
    unnamed x2 -> x0, waiting for transfers between devices: 89.5 us -> none
    all_to_all x1 -> x0, waiting for transfers between devices: 68.1 us -> none  [on_device(): lax.all_to_all(outbound.reshape(replicas, CAP, page_len, kv_local, 2 * HE...]
    pallas_call x0 -> x1, Pallas kernels: none -> 51.8 us  [on_device(): pl.pallas_call(functools.partial(kernel, R, T, B, NL, LOCAL, POOL, OUT, U...]
    all_gather x2 -> x0, blocking collectives: 28.6 us -> none  [the longest x1 14.6 us: on_device(): lax.all_gather(rms_norm(attended, ffn_gain), 'tensor', axis=0, tiled=True)]
    unnamed x1 -> x0, blocking collectives: 22.4 us -> none
    select_n x5 -> x0, other arithmetic: 20.3 us -> none  [the longest x1 15.6 us: on_device(): jnp.where(entries >= 0, jnp.clip(ctx_len[owners] - slot_idx * page_len, 0...]
    all_to_all x1 -> x0, starting transfers between devices: 17.5 us -> none  [on_device(): lax.all_to_all(outbound.reshape(replicas, CAP, page_len, kv_local, 2 * HE...]
    dot_general x11 -> x0, matrix products: 15.5 us -> none  [the longest x1 3.68 us: page_partials(): jnp.einsum('pkgt,ptkh->pkgh', weights.astype(jnp.bfloat16), page_rows[......]
  transfers between devices with their start and end apart: 2 -> 0, of which waited for: 2 -> 0; matrix products, arithmetic and copies ran while one was open for 11% -> 0% of each run, Pallas kernels for 0% -> 0%
where the time goes in v1:
time: 66.9 us; the launch traced here: 66.3 us
  Pallas kernels  51.8 us (77%)
  local copies, waits for them, and re-layouts  13.8 us (21%)
    pallas_call x1, Pallas kernels, on_device(): pl.pallas_call(functools.partial(kernel, R, T, B, NL, LOCAL, POOL, OUT, U...  51.8 us
    unnamed x26, local copies, waits for them, and re-layouts  12.4 us

profile of v1, /device:TPU:1, one launch (start us, length us, event | category | flops | bytes accessed | tf_op | source)
XLA Modules:
  0.0 66.3 jit_solution(7668951227140634635)
XLA Ops:
  0.6 0.7 %reshape.25.again = f32[1,1536]{1,0:T(1,128)S(1)} reshape(f32[1536]{0:T(1024)} %param.15) | data formatting | bytes 12288 | tf_op jit(solution)/shard_map/reshape | solution.py:455
  1.3 0.7 %reshape.30.fgain = f32[1,1536]{1,0:T(1,128)S(1)} reshape(f32[1536]{0:T(1024)} %param.23) | data formatting | bytes 12288 | tf_op jit(solution)/shard_map/reshape | solution.py:463
  2.0 0.0 copy-start
  2.0 1.7 %copy-done = bf16[72,128,1,128]{3,1,2,0:T(8,128)(2,1)S(1)} copy-done((bf16[72,128,1,128]{3,1,2,0:T(8,128)(2,1)S(1)}, bf16[72,128,1,128]{3,1,2,0:T(8,128)(2,1)}, u32[]{:S(2)}) %copy-start) | copy-done | bytes 2359320
  3.7 0.0 copy-start.1
  3.7 1.1 %copy-done.1 = bf16[1536,2,128]{2,1,0:T(2,128)(2,1)S(1)} copy-done((bf16[1536,2,128]{2,1,0:T(2,128)(2,1)S(1)}, bf16[1536,2,128]{2,1,0:T(2,128)(2,1)}, u32[]{:S(2)}) %copy-start.1) | copy-done | bytes 786456
  4.8 0.0 copy-start.2
  4.8 1.1 %copy-done.2 = bf16[1536,192]{0,1:T(8,128)(2,1)S(1)} copy-done((bf16[1536,192]{0,1:T(8,128)(2,1)S(1)}, bf16[1536,192]{0,1:T(8,128)(2,1)}, u32[]{:S(2)}) %copy-start.2) | copy-done | bytes 589848
  5.9 0.0 copy-start.3
  5.9 1.1 %copy-done.3 = bf16[192,1536]{1,0:T(8,128)(2,1)S(1)} copy-done((bf16[192,1536]{1,0:T(8,128)(2,1)S(1)}, bf16[192,1536]{1,0:T(8,128)(2,1)}, u32[]{:S(2)}) %copy-start.3) | copy-done | bytes 589848
  7.0 0.0 copy-start.4
  7.0 1.0 %copy-done.4 = bf16[1536,1,128]{2,0,1:T(8,128)(2,1)S(1)} copy-done((bf16[1536,1,128]{2,0,1:T(8,128)(2,1)S(1)}, bf16[1536,1,128]{2,0,1:T(8,128)(2,1)}, u32[]{:S(2)}) %copy-start.4) | copy-done | bytes 393240
  8.0 1.0 %copy-done.5 = bf16[128,1536]{1,0:T(8,128)(2,1)S(1)} copy-done((bf16[128,1536]{1,0:T(8,128)(2,1)S(1)}, bf16[128,1536]{1,0:T(8,128)(2,1)}, u32[]{:S(2)}) %copy-start.5) | copy-done | bytes 393240
  9.0 0.0 copy-start.6
  9.0 0.9 %copy-done.6 = bf16[1536,40]{0,1:T(8,128)(2,1)S(1)} copy-done((bf16[1536,40]{0,1:T(8,128)(2,1)S(1)}, bf16[1536,40]{0,1:T(8,128)(2,1)}, u32[]{:S(2)}) %copy-start.6) | copy-done | bytes 122904
  9.9 0.0 copy-start.7
  9.9 0.7 %copy-done.7 = bf16[4,1536]{1,0:T(4,128)(2,1)S(1)} copy-done((bf16[4,1536]{1,0:T(4,128)(2,1)S(1)}, bf16[4,1536]{1,0:T(4,128)(2,1)}, u32[]{:S(2)}) %copy-start.7) | copy-done | bytes 12312
  10.6 0.7 %copy-done.8 = s32[32,16]{0,1:T(8,128)S(1)} copy-done((s32[32,16]{0,1:T(8,128)S(1)}, s32[32,16]{0,1:T(8,128)}, u32[]{:S(2)}) %copy-start.8) | copy-done | bytes 2072
  11.3 0.7 %copy-done.9 = s32[32,8]{0,1:T(8,128)S(1)} copy-done((s32[32,8]{0,1:T(8,128)S(1)}, s32[32,8]{0,1:T(8,128)}, u32[]{:S(2)}) %copy-start.9) | copy-done | bytes 1048
  12.0 0.7 copy-done.10
  12.6 0.7 copy-done.11
  13.3 51.8 %decode_step.1 = (bf16[4,1536]{1,0:T(4,128)(2,1)S(1)}, bf16[4,1536]{1,0:T(4,128)(2,1)S(1)}) custom-call(bf16[4,1536]{1,0:T(4,128)(2,1)S(1)} %copy-done.7, f32[1,1536]{1,0:T(1,128)S(1)} %reshape.25.again, bf16[192,1536]{1,0:T(8,128)(2,1)S(1)} %bitcast.11, bf16[1536,128]{1,0:T(8,128)(2,1)S(1)} %bitcast.12, bf16[192,1536]{1,0:T(8,128)(2,1)S(1)} %copy-done.3, ...), custom_call_target="tpu_custom_call" | custom-call | tf_op jit(solution)/shard_map/decode_step/pallas_call | solution.py:503
  65.1 0.6 copy.18
  65.7 0.6 copy.19
  (5 shorter events, 0.0 us)
Async XLA Ops:
  2.0 1.7 %copy-start = (bf16[72,128,1,128]{3,1,2,0:T(8,128)(2,1)S(1)}, bf16[72,128,1,128]{3,1,2,0:T(8,128)(2,1)}, u32[]{:S(2)}) copy-start(bf16[72,128,1,128]{3,1,2,0:T(8,128)(2,1)} %param.19) | copy-start | bytes 7077892
  3.7 1.1 %copy-start.1 = (bf16[1536,2,128]{2,1,0:T(2,128)(2,1)S(1)}, bf16[1536,2,128]{2,1,0:T(2,128)(2,1)}, u32[]{:S(2)}) copy-start(bf16[1536,2,128]{2,1,0:T(2,128)(2,1)} %param.26) | copy-start | bytes 2359300
  4.8 1.1 %copy-start.2 = (bf16[1536,192]{0,1:T(8,128)(2,1)S(1)}, bf16[1536,192]{0,1:T(8,128)(2,1)}, u32[]{:S(2)}) copy-start(bf16[1536,192]{0,1:T(8,128)(2,1)} %param.16) | copy-start | bytes 1769476
  5.9 1.1 %copy-start.3 = (bf16[192,1536]{1,0:T(8,128)(2,1)S(1)}, bf16[192,1536]{1,0:T(8,128)(2,1)}, u32[]{:S(2)}) copy-start(bf16[192,1536]{1,0:T(8,128)(2,1)} %wo.1) | copy-start | bytes 1769476
  7.0 1.0 %copy-start.4 = (bf16[1536,1,128]{2,0,1:T(8,128)(2,1)S(1)}, bf16[1536,1,128]{2,0,1:T(8,128)(2,1)}, u32[]{:S(2)}) copy-start(bf16[1536,1,128]{2,0,1:T(8,128)(2,1)} %param.17) | copy-start | bytes 1179652
  8.0 1.0 %copy-start.5 = (bf16[128,1536]{1,0:T(8,128)(2,1)S(1)}, bf16[128,1536]{1,0:T(8,128)(2,1)}, u32[]{:S(2)}) copy-start(bf16[128,1536]{1,0:T(8,128)(2,1)} %wdown.1) | copy-start | bytes 1179652
  9.0 0.9 %copy-start.6 = (bf16[1536,40]{0,1:T(8,128)(2,1)S(1)}, bf16[1536,40]{0,1:T(8,128)(2,1)}, u32[]{:S(2)}) copy-start(bf16[1536,40]{0,1:T(8,128)(2,1)} %param.24) | copy-start | bytes 368644
  9.9 0.7 %copy-start.7 = (bf16[4,1536]{1,0:T(4,128)(2,1)S(1)}, bf16[4,1536]{1,0:T(4,128)(2,1)}, u32[]{:S(2)}) copy-start(bf16[4,1536]{1,0:T(4,128)(2,1)} %hid.1) | copy-start | bytes 36868
  10.6 0.7 %copy-start.8 = (s32[32,16]{0,1:T(8,128)S(1)}, s32[32,16]{0,1:T(8,128)}, u32[]{:S(2)}) copy-start(s32[32,16]{0,1:T(8,128)} %param.20) | copy-start | bytes 6148
  11.3 0.7 %copy-start.9 = (s32[32,8]{0,1:T(8,128)S(1)}, s32[32,8]{0,1:T(8,128)}, u32[]{:S(2)}) copy-start(s32[32,8]{0,1:T(8,128)} %param.25) | copy-start | bytes 3076
  11.9 0.7 copy-start.10
  12.6 0.7 copy-start.11

commit v2 on v1

--- a/solution.py
+++ b/solution.py
@@ -96,11 +96,11 @@
 def kernel(
     R, T, B, NL, LOCAL, POOL, OUT, UNITS,
     hid, again, wq, wkv, wo, cache, ptab, ctx, mdest, fgain, router, routes, win, wdown,
-    att_o, exp_o,
+    both_o,
     hid_v, again_v, wq_v, wkv_v, wo_v, cache_v, ptab_v, ctx_v, mdest_v, fgain_v, router_v,
-    routes_v, win_v, wdown_v, win_f, wgu_v, fold_v, a1_v, qg_v, loc_v, att_v, exp_v,
+    routes_v, win_v, wdown_v, win_f, wgu_v, fold_v, a1_v, qg_v, loc_v,
     xg, msg, inq, ret_s, ret, rs_s, rs, fg, es_s, es,
-    isem, osem, ready, ssem, rsem,
+    isem, ready, ssem, rsem,
 ):
     r = lax.axis_index("replica")
     t = lax.axis_index("tensor")
@@ -110,6 +110,17 @@
     y, z = r // NZ, lax.rem(r, NZ)
     NIN = R * ROWS
     NR = GROUPS * B
+
+    barrier = pltpu.get_barrier_semaphore()
+    for k in range(1, T):
+        pl.semaphore_signal(barrier, inc=1, device_id=(r, lax.rem(t + k, T)), device_id_type=MESH)
+    for k in range(1, NZ):
+        pl.semaphore_signal(
+            barrier, inc=1, device_id=(lax.rem(y + k, NZ) * NZ + z, t), device_id_type=MESH
+        )
+        pl.semaphore_signal(
+            barrier, inc=1, device_id=(y * NZ + lax.rem(z + k, NZ), t), device_id_type=MESH
+        )
 
     loads = []
 
@@ -134,17 +145,6 @@
     get_routes = load(routes, routes_v)
     get_fgain = load(fgain, fgain_v)
 
-    barrier = pltpu.get_barrier_semaphore()
-    for k in range(1, T):
-        pl.semaphore_signal(barrier, inc=1, device_id=(r, lax.rem(t + k, T)), device_id_type=MESH)
-    for k in range(1, NZ):
-        pl.semaphore_signal(
-            barrier, inc=1, device_id=(lax.rem(y + k, NZ) * NZ + z, t), device_id_type=MESH
-        )
-        pl.semaphore_signal(
-            barrier, inc=1, device_id=(y * NZ + lax.rem(z + k, NZ), t), device_id_type=MESH
-        )
-
     low8 = iota((8, H), 0) < 4
 
     def normalise(folded, gain):
@@ -153,8 +153,8 @@
         return folded * lax.rsqrt(mean + EPSILON) * gain
 
     def fold_gain(ref):
-        left = jnp.broadcast_to(ref[:, 0:H], (8, H))
-        right = jnp.broadcast_to(ref[:, H:D], (8, H))
+        left = jnp.broadcast_to(ref[0:H].reshape(1, H), (8, H))
+        right = jnp.broadcast_to(ref[H:D].reshape(1, H), (8, H))
         return jnp.where(low8, left, right)
 
     get_hid.wait()
@@ -185,16 +185,18 @@
                 device_id=(r, peer), device_id_type=MESH,
             ).start()
 
+    offsets = sorted(
+        ((dy, dz) for dy in range(NZ) for dz in range(NZ) if dy or dz),
+        key=lambda d: -(min(d[0], NZ - d[0]) + min(d[1], NZ - d[1])),
+    )
+
     def exchange(src, dst, phase):
-        def step(k, carry):
-            peer = lax.rem(r + k, R)
+        for dy, dz in offsets:
+            peer = lax.rem(y + dy, NZ) * NZ + lax.rem(z + dz, NZ)
             pltpu.make_async_remote_copy(
                 src.at[peer], dst.at[r], ssem.at[phase], rsem.at[phase],
                 device_id=(peer, t), device_id_type=MESH,
             ).start()
-            return carry
-
-        lax.fori_loop(1, R, step, 0)
 
     def arrived(buf, sems, phase):
         part = buf.at[0 : buf.shape[0] - 1]
@@ -388,10 +390,8 @@
     attended_f = attended.astype(F32)
     fg[t] = normalise(attended_f, gain_f).astype(BF)
     share(fg, 4)
-    att_v[:, 0:H] = attended_f[0:4].astype(BF)
-    att_v[:, H:D] = attended_f[4:8].astype(BF)
-    put_att = pltpu.make_async_copy(att_v, att_o, osem.at[0])
-    put_att.start()
+    both_o[:, 0:H] = attended_f[0:4].astype(BF)
+    both_o[:, H:D] = attended_f[4:8].astype(BF)
 
     arrived(fg, rsem, 4)
     ffn = fg[...].astype(F32).reshape(T * 8, H).astype(BF)
@@ -413,14 +413,10 @@
     es[t] = es_s[t]
     arrived(es, rsem, 5)
     experts = jnp.sum(es[...].astype(F32), axis=0)
-    exp_v[:, 0:H] = experts[0:4].astype(BF)
-    exp_v[:, H:D] = experts[4:8].astype(BF)
-    put_exp = pltpu.make_async_copy(exp_v, exp_o, osem.at[1])
-    put_exp.start()
+    both_o[:, D : D + H] = experts[0:4].astype(BF)
+    both_o[:, D + H :] = experts[4:8].astype(BF)
     for phase, buf in enumerate((xg, inq, ret, rs, fg, es)):
         arrived(buf, ssem, phase)
-    put_att.wait()
-    put_exp.wait()
 
 
 def on_device(
@@ -452,7 +448,7 @@
     NIN = R * ROWS
     args = (
         hidden,
-        attn_gain.reshape(1, D),
+        attn_gain,
         w_query.T,
         w_keyvalue.reshape(D, 2 * HEAD_DIM),
         w_output,
@@ -460,7 +456,7 @@
         page_table.T,
         ctx_len.reshape(1, B),
         move_dest.reshape(1, OUT),
-        ffn_gain.reshape(1, D),
+        ffn_gain,
         router.T,
         routes.T,
         w_in.reshape(2 * D, UNITS),
@@ -471,7 +467,7 @@
     landing[2] = vm((256, D), BF)
     landing[4] = vm((256, D), BF)
     landing[10] = vm((128, D), BF)
-    any_spec = pl.BlockSpec(memory_space=pl.ANY)
+    any_spec = pl.BlockSpec(memory_space=pltpu.HBM)
     group = vm((T, 8, H), BF)
     inbox = vm((R, ROWS, 128), BF)
     scratch = landing + [
@@ -481,8 +477,6 @@
         vm((NL + NIN, 4 * B), BF),
         vm((4 * B, 128), BF),
         vm((NL, 128), BF),
-        vm((4, D), BF),
-        vm((4, D), BF),
         group,
         inbox,
         inbox,
@@ -494,23 +488,22 @@
         group,
         group,
         pltpu.SemaphoreType.DMA((len(args),)),
-        pltpu.SemaphoreType.DMA((2,)),
         pltpu.SemaphoreType.REGULAR,
         pltpu.SemaphoreType.DMA((6,)),
         pltpu.SemaphoreType.DMA((6,)),
     ]
-    shape = jax.ShapeDtypeStruct((4, D), BF)
-    return pl.pallas_call(
+    both = pl.pallas_call(
         functools.partial(kernel, R, T, B, NL, LOCAL, POOL, OUT, UNITS),
-        out_shape=(shape, shape),
+        out_shape=pltpu.VMEM((4, 2 * D), BF),
         in_specs=[any_spec] * len(args),
-        out_specs=(any_spec, any_spec),
+        out_specs=pl.BlockSpec(memory_space=pltpu.VMEM),
         scratch_shapes=scratch,
         name="decode_step",
         compiler_params=pltpu.CompilerParams(
             collective_id=0, has_side_effects=True, vmem_limit_bytes=32 * 1024 * 1024
         ),
-    )(*args)
+    )(*[pltpu.with_memory_space_constraint(a, pltpu.HBM) for a in args])
+    return both[:, 0:D], both[:, D:]
 
 
 def solution(mesh):

time: 66.9 us -> 49.6 us (0.74)
  local copies, waits for them, and re-layouts: 13.8 us -> 0.61 us
  Pallas kernels: 51.8 us -> 48.1 us
    unnamed x26 -> x0, local copies, waits for them, and re-layouts: 12.4 us -> none
    pallas_call x1, Pallas kernels: 51.8 us -> 48.1 us  [on_device(): pl.pallas_call(functools.partial(kernel, R, T, B, NL, LOCAL, POOL, OUT, U...]
    reshape x2 -> x0, local copies, waits for them, and re-layouts: 1.4 us -> none  [the longest x1 0.7 us: on_device(): attn_gain.reshape(1, D)]
where the time goes in v2:
time: 49.6 us; the launch traced here: 49.4 us
  Pallas kernels  48.1 us (97%)
  between operations  0.64 us (1%)
  local copies, waits for them, and re-layouts  0.61 us (1%)
    pallas_call x1, Pallas kernels, on_device(): pl.pallas_call(functools.partial(kernel, R, T, B, NL, LOCAL, POOL, OUT, U...  48.1 us

profile of v2, /device:TPU:1, one launch (start us, length us, event | category | flops | bytes accessed | tf_op | source)
XLA Modules:
  0.0 49.4 jit_solution(16405502419807242730)
XLA Ops:
  0.6 48.1 %decode_step.1 = bf16[4,3072]{1,0:T(4,128)(2,1)S(1)} custom-call(bf16[4,1536]{1,0:T(4,128)(2,1)} %hid.1, f32[1536]{0:T(1024)} %again.1, bf16[192,1536]{1,0:T(8,128)(2,1)} %bitcast.11, bf16[1536,128]{1,0:T(8,128)(2,1)} %bitcast.12, bf16[192,1536]{1,0:T(8,128)(2,1)} %wo.1, bf16[72,128,128]{2,1,0:T(8,128)(2,1)} %bitcast.9, s32[16,32]{1,0:T(8,128)} %bitcast.14, ...), custom_call_target="tpu_custom_call" | custom-call | tf_op jit(solution)/shard_map/decode_step/pallas_call | solution.py:495
  48.8 0.6 %fusion = (bf16[4,1536]{1,0:T(4,128)(2,1)}, bf16[4,1536]{1,0:T(4,128)(2,1)}) fusion(bf16[4,3072]{1,0:T(4,128)(2,1)S(1)} %decode_step.1), kind=kLoop, calls=%fused_computation | loop fusion | bytes 49152 | tf_op jit(solution)/shard_map/slice | solution.py:506

commit v3 on v2

--- a/solution.py
+++ b/solution.py
@@ -111,6 +111,17 @@
     NIN = R * ROWS
     NR = GROUPS * B
 
+    loads = []
+
+    def load(src, dst):
+        copy = pltpu.make_async_copy(src, dst, isem.at[len(loads)])
+        copy.start()
+        loads.append(copy)
+        return copy
+
+    get_hid = load(hid, hid_v)
+    get_again = load(again, again_v)
+
     barrier = pltpu.get_barrier_semaphore()
     for k in range(1, T):
         pl.semaphore_signal(barrier, inc=1, device_id=(r, lax.rem(t + k, T)), device_id_type=MESH)
@@ -122,16 +133,71 @@
             barrier, inc=1, device_id=(y * NZ + lax.rem(z + k, NZ), t), device_id_type=MESH
         )
 
-    loads = []
-
-    def load(src, dst):
-        copy = pltpu.make_async_copy(src, dst, isem.at[len(loads)])
-        copy.start()
-        loads.append(copy)
-        return copy
-
-    get_hid = load(hid, hid_v)
-    get_again = load(again, again_v)
+    low8 = iota((8, H), 0) < 4
+
+    def normalise(folded, gain):
+        squares = jnp.sum(folded * folded, axis=1, keepdims=True)
+        mean = (squares + roll4(jnp.broadcast_to(squares, (8, 128)))[:, 0:1]) * (1.0 / D)
+        return folded * lax.rsqrt(mean + EPSILON) * gain
+
+    def fold_gain(ref):
+        left = jnp.broadcast_to(ref[0:H].reshape(1, H), (8, H))
+        right = jnp.broadcast_to(ref[H:D].reshape(1, H), (8, H))
+        return jnp.where(low8, left, right)
+
+    get_hid.wait()
+    get_again.wait()
+    hidden = hid_v[...].astype(F32)
+    fold_v[0:4, :] = hidden[:, 0:H]
+    fold_v[4:8, :] = hidden[:, H:D]
+    xg[t] = normalise(fold_v[...], fold_gain(again_v)).astype(BF)
+
+    pl.semaphore_wait(barrier, (T - 1) + 2 * (NZ - 1))
+    chip, core, chips = t // 2, lax.rem(t, 2), T // 2
+    steps = sorted(range(chips), key=lambda d: (-min(d, chips - d), d))
+    peers = [
+        lax.rem(chip + d, chips) * 2 + (core if same else 1 - core)
+        for d in steps
+        for same in (1, 0)
+        if d or not same
+    ]
+
+    def share(buf, phase):
+        for peer in peers:
+            pltpu.make_async_remote_copy(
+                buf.at[t], buf.at[t], ssem.at[phase], rsem.at[phase],
+                device_id=(r, peer), device_id_type=MESH,
+            ).start()
+
+    def scatter(src, dst, phase):
+        for peer in peers:
+            pltpu.make_async_remote_copy(
+                src.at[peer], dst.at[t], ssem.at[phase], rsem.at[phase],
+                device_id=(r, peer), device_id_type=MESH,
+            ).start()
+
+    offsets = sorted(
+        ((dy, dz) for dy in range(NZ) for dz in range(NZ) if dy or dz),
+        key=lambda d: -(min(d[0], NZ - d[0]) + min(d[1], NZ - d[1])),
+    )
+
+    def exchange(src, dst, phase):
+        for dy, dz in offsets:
+            peer = lax.rem(y + dy, NZ) * NZ + lax.rem(z + dz, NZ)
+            pltpu.make_async_remote_copy(
+                src.at[peer], dst.at[r], ssem.at[phase], rsem.at[phase],
+                device_id=(peer, t), device_id_type=MESH,
+            ).start()
+
+    def arrived(buf, sems, phase):
+        part = buf.at[0 : buf.shape[0] - 1]
+        pltpu.make_async_copy(part, part, sems.at[phase]).wait()
+
+    share(xg, 0)
+    for k in range(1, NZ):
+        pl.semaphore_signal(
+            ready, inc=1, device_id=(y * NZ + lax.rem(z + k, NZ), t), device_id_type=MESH
+        )
     get_ptab = load(ptab, ptab_v)
     get_ctx = load(ctx, ctx_v)
     get_mdest = load(mdest, mdest_v)
@@ -144,65 +210,6 @@
     get_router = load(router, router_v.at[0:EXPERTS])
     get_routes = load(routes, routes_v)
     get_fgain = load(fgain, fgain_v)
-
-    low8 = iota((8, H), 0) < 4
-
-    def normalise(folded, gain):
-        squares = jnp.sum(folded * folded, axis=1, keepdims=True)
-        mean = (squares + roll4(jnp.broadcast_to(squares, (8, 128)))[:, 0:1]) * (1.0 / D)
-        return folded * lax.rsqrt(mean + EPSILON) * gain
-
-    def fold_gain(ref):
-        left = jnp.broadcast_to(ref[0:H].reshape(1, H), (8, H))
-        right = jnp.broadcast_to(ref[H:D].reshape(1, H), (8, H))
-        return jnp.where(low8, left, right)
-
-    get_hid.wait()
-    get_again.wait()
-    hidden = hid_v[...].astype(F32)
-    fold_v[0:4, :] = hidden[:, 0:H]
-    fold_v[4:8, :] = hidden[:, H:D]
-    xg[t] = normalise(fold_v[...], fold_gain(again_v)).astype(BF)
-
-    pl.semaphore_wait(barrier, (T - 1) + 2 * (NZ - 1))
-    for k in range(1, NZ):
-        pl.semaphore_signal(
-            ready, inc=1, device_id=(y * NZ + lax.rem(z + k, NZ), t), device_id_type=MESH
-        )
-
-    def share(buf, phase):
-        for k in range(1, T):
-            pltpu.make_async_remote_copy(
-                buf.at[t], buf.at[t], ssem.at[phase], rsem.at[phase],
-                device_id=(r, lax.rem(t + k, T)), device_id_type=MESH,
-            ).start()
-
-    def scatter(src, dst, phase):
-        for k in range(1, T):
-            peer = lax.rem(t + k, T)
-            pltpu.make_async_remote_copy(
-                src.at[peer], dst.at[t], ssem.at[phase], rsem.at[phase],
-                device_id=(r, peer), device_id_type=MESH,
-            ).start()
-
-    offsets = sorted(
-        ((dy, dz) for dy in range(NZ) for dz in range(NZ) if dy or dz),
-        key=lambda d: -(min(d[0], NZ - d[0]) + min(d[1], NZ - d[1])),
-    )
-
-    def exchange(src, dst, phase):
-        for dy, dz in offsets:
-            peer = lax.rem(y + dy, NZ) * NZ + lax.rem(z + dz, NZ)
-            pltpu.make_async_remote_copy(
-                src.at[peer], dst.at[r], ssem.at[phase], rsem.at[phase],
-                device_id=(peer, t), device_id_type=MESH,
-            ).start()
-
-    def arrived(buf, sems, phase):
-        part = buf.at[0 : buf.shape[0] - 1]
-        pltpu.make_async_copy(part, part, sems.at[phase]).wait()
-
-    share(xg, 0)
 
     get_ptab.wait()
     get_ctx.wait()

time: 49.6 us -> 49.1 us (0.990)
  Pallas kernels: 48.1 us -> 47.5 us
    pallas_call x1, Pallas kernels: 48.1 us -> 47.5 us  [on_device(): pl.pallas_call(functools.partial(kernel, R, T, B, NL, LOCAL, POOL, OUT, U...]
where the time goes in v3:
time: 49.1 us; the launch traced here: 48.8 us
  Pallas kernels  47.5 us (97%)
  between operations  0.64 us (1%)
  local copies, waits for them, and re-layouts  0.61 us (1%)
    pallas_call x1, Pallas kernels, on_device(): pl.pallas_call(functools.partial(kernel, R, T, B, NL, LOCAL, POOL, OUT, U...  47.5 us

profile of v3, /device:TPU:1, one launch (start us, length us, event | category | flops | bytes accessed | tf_op | source)
XLA Modules:
  0.0 48.8 jit_solution(9610014216764843051)
XLA Ops:
  0.6 47.5 %decode_step.1 = bf16[4,3072]{1,0:T(4,128)(2,1)S(1)} custom-call(bf16[4,1536]{1,0:T(4,128)(2,1)} %hid.1, f32[1536]{0:T(1024)} %again.1, bf16[192,1536]{1,0:T(8,128)(2,1)} %bitcast.11, bf16[1536,128]{1,0:T(8,128)(2,1)} %bitcast.12, bf16[192,1536]{1,0:T(8,128)(2,1)} %wo.1, bf16[72,128,128]{2,1,0:T(8,128)(2,1)} %bitcast.9, s32[16,32]{1,0:T(8,128)} %bitcast.14, ...), custom_call_target="tpu_custom_call" | custom-call | tf_op jit(solution)/shard_map/decode_step/pallas_call | solution.py:502
  48.2 0.6 %fusion = (bf16[4,1536]{1,0:T(4,128)(2,1)}, bf16[4,1536]{1,0:T(4,128)(2,1)}) fusion(bf16[4,3072]{1,0:T(4,128)(2,1)S(1)} %decode_step.1), kind=kLoop, calls=%fused_computation | loop fusion | bytes 49152 | tf_op jit(solution)/shard_map/slice | solution.py:513

commit v4 on v3

--- a/solution.py
+++ b/solution.py
@@ -87,9 +87,10 @@
         preferred_element_type=F32,
     ).reshape(count * 8, 128)
     coarse = top.astype(BF).astype(F32)
-    rows = jnp.where(
-        lane < 16, coarse, jnp.where(lane < 32, top - coarse, jnp.where(lane < 64, total, out))
-    )
+    middle = (top - coarse).astype(BF).astype(F32)
+    fine = top - coarse - middle
+    rows = jnp.where(lane < 16, middle, jnp.where(lane < 32, fine, jnp.where(lane < 64, total, out)))
+    rows = jnp.where(lane < 8, coarse, rows)
     return rows.astype(BF)
 
 
@@ -125,7 +126,8 @@
     barrier = pltpu.get_barrier_semaphore()
     for k in range(1, T):
         pl.semaphore_signal(barrier, inc=1, device_id=(r, lax.rem(t + k, T)), device_id_type=MESH)
-    for k in range(1, NZ):
+    ring = sorted(range(1, NZ), key=lambda d: -min(d, NZ - d))
+    for k in ring:
         pl.semaphore_signal(
             barrier, inc=1, device_id=(lax.rem(y + k, NZ) * NZ + z, t), device_id_type=MESH
         )
@@ -193,11 +195,11 @@
         part = buf.at[0 : buf.shape[0] - 1]
         pltpu.make_async_copy(part, part, sems.at[phase]).wait()
 
-    share(xg, 0)
-    for k in range(1, NZ):
+    for k in ring:
         pl.semaphore_signal(
             ready, inc=1, device_id=(y * NZ + lax.rem(z + k, NZ), t), device_id_type=MESH
         )
+    share(xg, 0)
     get_ptab = load(ptab, ptab_v)
     get_ctx = load(ctx, ctx_v)
     get_mdest = load(mdest, mdest_v)
@@ -303,7 +305,7 @@
     get_wkv.wait()
 
     arrived(xg, rsem, 0)
-    normed = xg[...].astype(F32).reshape(T * 8, H).astype(BF)
+    normed = xg[...].reshape(T * 8, H)
     q_all = [mm_t(normed, wq_v[:, c * H : (c + 1) * H]) for c in range(2)]
     kv_all = [mm(normed, wkv_v[c * H : (c + 1) * H, :]) for c in range(2)]
     q01 = rotate(unfold(q_all[0][:, 0:128], q_all[1][:, 0:128], T))
@@ -332,7 +334,7 @@
     owned_loc = mm_t(eye, a1_v[0:NL, :])[0:NR] > 0.5
     owned_in = mm_t(eye, a1_v[NL:, :])[0:NR] > 0.5
     lane_sel = iota((NR, 128), 1)
-    max_sel = jnp.where((lane_sel == 0) | (lane_sel == 16), 1.0, 0.0).astype(BF)
+    max_sel = jnp.where((lane_sel == 0) | (lane_sel == 8) | (lane_sel == 16), 1.0, 0.0).astype(BF)
     new_key = rotate(new_kv)
     new_score = jnp.concatenate(
         [jnp.sum(h * new_key, axis=1, keepdims=True) for h in heads], axis=0
@@ -348,7 +350,7 @@
     place = place_map()
 
     arrived(inq, rsem, 1)
-    sent = inq[...].astype(F32).reshape(NIN, 128).astype(BF)
+    sent = inq[...].reshape(NIN, 128)
     lent = page_rows(mm(fetch, sent), cache_v[LOCAL:POOL])
     ret_s[...] = mm(place, lent).reshape(R, ROWS, 128).astype(BF)
     exchange(ret_s, ret, 2)
@@ -374,7 +376,7 @@
     residual = fold_v[...]
 
     arrived(ret, rsem, 2)
-    back = ret[...].astype(F32).reshape(NIN, 128).astype(BF)
+    back = ret[...].reshape(NIN, 128)
     score_in = jnp.where(owned_in, mm_t(max_sel, back), NEG_FILL)
     top = jnp.maximum(top_loc, jnp.max(score_in, axis=1, keepdims=True))
     merged = jnp.exp(top_loc - top) * sum_loc + mm(jnp.exp(score_in - top).astype(BF), back)
@@ -401,7 +403,7 @@
     both_o[:, H:D] = attended_f[4:8].astype(BF)
 
     arrived(fg, rsem, 4)
-    ffn = fg[...].astype(F32).reshape(T * 8, H).astype(BF)
+    ffn = fg[...].reshape(T * 8, H)
     up_all = [mm(ffn, wgu_v[c * H : (c + 1) * H, :]) for c in range(2)]
     log_all = [mm_t(ffn, router_v[:, c * H : (c + 1) * H]) for c in range(2)]
     gate = unfold(up_all[0][:, 0:UNITS], up_all[1][:, 0:UNITS], T)

time: 49.1 us -> 49.1 us (level)
  no operation moved by 1% of the time
where the time goes in v4:
time: 49.1 us; the launch traced here: 48.8 us
  Pallas kernels  47.5 us (97%)
  between operations  0.64 us (1%)
  local copies, waits for them, and re-layouts  0.61 us (1%)
    pallas_call x1, Pallas kernels, on_device(): pl.pallas_call(functools.partial(kernel, R, T, B, NL, LOCAL, POOL, OUT, U...  47.5 us

profile of v4, /device:TPU:1, one launch (start us, length us, event | category | flops | bytes accessed | tf_op | source)
XLA Modules:
  0.0 48.8 jit_solution(3662274357799595410)
XLA Ops:
  0.6 47.5 %decode_step.1 = bf16[4,3072]{1,0:T(4,128)(2,1)S(1)} custom-call(bf16[4,1536]{1,0:T(4,128)(2,1)} %hid.1, f32[1536]{0:T(1024)} %again.1, bf16[192,1536]{1,0:T(8,128)(2,1)} %bitcast.11, bf16[1536,128]{1,0:T(8,128)(2,1)} %bitcast.12, bf16[192,1536]{1,0:T(8,128)(2,1)} %wo.1, bf16[72,128,128]{2,1,0:T(8,128)(2,1)} %bitcast.9, s32[16,32]{1,0:T(8,128)} %bitcast.14, ...), custom_call_target="tpu_custom_call" | custom-call | tf_op jit(solution)/shard_map/decode_step/pallas_call | solution.py:504
  48.2 0.6 %fusion = (bf16[4,1536]{1,0:T(4,128)(2,1)}, bf16[4,1536]{1,0:T(4,128)(2,1)}) fusion(bf16[4,3072]{1,0:T(4,128)(2,1)S(1)} %decode_step.1), kind=kLoop, calls=%fused_computation | loop fusion | bytes 49152 | tf_op jit(solution)/shard_map/slice | solution.py:515

commit v5 on v4

--- a/solution.py
+++ b/solution.py
@@ -124,16 +124,17 @@
     get_again = load(again, again_v)
 
     barrier = pltpu.get_barrier_semaphore()
-    for k in range(1, T):
-        pl.semaphore_signal(barrier, inc=1, device_id=(r, lax.rem(t + k, T)), device_id_type=MESH)
     ring = sorted(range(1, NZ), key=lambda d: -min(d, NZ - d))
     for k in ring:
         pl.semaphore_signal(
             barrier, inc=1, device_id=(lax.rem(y + k, NZ) * NZ + z, t), device_id_type=MESH
         )
+    for k in ring:
         pl.semaphore_signal(
             barrier, inc=1, device_id=(y * NZ + lax.rem(z + k, NZ), t), device_id_type=MESH
         )
+    for k in range(1, T):
+        pl.semaphore_signal(barrier, inc=1, device_id=(r, lax.rem(t + k, T)), device_id_type=MESH)
 
     low8 = iota((8, H), 0) < 4
 
@@ -195,11 +196,11 @@
         part = buf.at[0 : buf.shape[0] - 1]
         pltpu.make_async_copy(part, part, sems.at[phase]).wait()
 
-    for k in ring:
+    share(xg, 0)
+    for k in range(1, NZ):
         pl.semaphore_signal(
             ready, inc=1, device_id=(y * NZ + lax.rem(z + k, NZ), t), device_id_type=MESH
         )
-    share(xg, 0)
     get_ptab = load(ptab, ptab_v)
     get_ctx = load(ctx, ctx_v)
     get_mdest = load(mdest, mdest_v)
@@ -305,7 +306,7 @@
     get_wkv.wait()
 
     arrived(xg, rsem, 0)
-    normed = xg[...].reshape(T * 8, H)
+    normed = xg[...].astype(F32).reshape(T * 8, H).astype(BF)
     q_all = [mm_t(normed, wq_v[:, c * H : (c + 1) * H]) for c in range(2)]
     kv_all = [mm(normed, wkv_v[c * H : (c + 1) * H, :]) for c in range(2)]
     q01 = rotate(unfold(q_all[0][:, 0:128], q_all[1][:, 0:128], T))
@@ -350,7 +351,7 @@
     place = place_map()
 
     arrived(inq, rsem, 1)
-    sent = inq[...].reshape(NIN, 128)
+    sent = inq[...].astype(F32).reshape(NIN, 128).astype(BF)
     lent = page_rows(mm(fetch, sent), cache_v[LOCAL:POOL])
     ret_s[...] = mm(place, lent).reshape(R, ROWS, 128).astype(BF)
     exchange(ret_s, ret, 2)
@@ -376,7 +377,7 @@
     residual = fold_v[...]
 
     arrived(ret, rsem, 2)
-    back = ret[...].reshape(NIN, 128)
+    back = ret[...].astype(F32).reshape(NIN, 128).astype(BF)
     score_in = jnp.where(owned_in, mm_t(max_sel, back), NEG_FILL)
     top = jnp.maximum(top_loc, jnp.max(score_in, axis=1, keepdims=True))
     merged = jnp.exp(top_loc - top) * sum_loc + mm(jnp.exp(score_in - top).astype(BF), back)
@@ -403,7 +404,7 @@
     both_o[:, H:D] = attended_f[4:8].astype(BF)
 
     arrived(fg, rsem, 4)
-    ffn = fg[...].reshape(T * 8, H)
+    ffn = fg[...].astype(F32).reshape(T * 8, H).astype(BF)
     up_all = [mm(ffn, wgu_v[c * H : (c + 1) * H, :]) for c in range(2)]
     log_all = [mm_t(ffn, router_v[:, c * H : (c + 1) * H]) for c in range(2)]
     gate = unfold(up_all[0][:, 0:UNITS], up_all[1][:, 0:UNITS], T)

time: 49.1 us -> 48.9 us (level)
  no operation moved by 1% of the time
where the time goes in v5:
time: 48.9 us; the launch traced here: 48.6 us
  Pallas kernels  47.4 us (97%)
  between operations  0.64 us (1%)
  local copies, waits for them, and re-layouts  0.61 us (1%)
    pallas_call x1, Pallas kernels, on_device(): pl.pallas_call(functools.partial(kernel, R, T, B, NL, LOCAL, POOL, OUT, U...  47.4 us

profile of v5, /device:TPU:1, one launch (start us, length us, event | category | flops | bytes accessed | tf_op | source)
XLA Modules:
  0.0 48.6 jit_solution(12130046198765257776)
XLA Ops:
  0.6 47.4 %decode_step.1 = bf16[4,3072]{1,0:T(4,128)(2,1)S(1)} custom-call(bf16[4,1536]{1,0:T(4,128)(2,1)} %hid.1, f32[1536]{0:T(1024)} %again.1, bf16[192,1536]{1,0:T(8,128)(2,1)} %bitcast.11, bf16[1536,128]{1,0:T(8,128)(2,1)} %bitcast.12, bf16[192,1536]{1,0:T(8,128)(2,1)} %wo.1, bf16[72,128,128]{2,1,0:T(8,128)(2,1)} %bitcast.9, s32[16,32]{1,0:T(8,128)} %bitcast.14, ...), custom_call_target="tpu_custom_call" | custom-call | tf_op jit(solution)/shard_map/decode_step/pallas_call | solution.py:505
  48.0 0.6 %fusion = (bf16[4,1536]{1,0:T(4,128)(2,1)}, bf16[4,1536]{1,0:T(4,128)(2,1)}) fusion(bf16[4,3072]{1,0:T(4,128)(2,1)S(1)} %decode_step.1), kind=kLoop, calls=%fused_computation | loop fusion | bytes 49152 | tf_op jit(solution)/shard_map/slice | solution.py:516

commit v6 on v5

--- a/solution.py
+++ b/solution.py
@@ -67,7 +67,7 @@
     return jnp.concatenate(first, axis=0).astype(BF), jnp.concatenate(second, axis=0).astype(BF)
 
 
-def page_rows(q_rows, pages):
+def page_rows(q_rows, pages, values):
     count = pages.shape[0]
     lane = iota((count * 8, 128), 1)
     span = jnp.where(lane < 64, pltpu.roll(q_rows, 64, 1), q_rows)
@@ -79,17 +79,16 @@
     scores = jnp.where(in_range, scores, NEG_FILL)
     top = jnp.max(scores, axis=1, keepdims=True)
     weights = jnp.where(in_range, jnp.exp(scores - top), 0.0)
-    total = jnp.sum(weights, axis=1, keepdims=True)
     out = lax.dot_general(
         weights.reshape(count, 8, 128).astype(BF),
-        pages,
+        values,
         (((2,), (1,)), ((0,), (0,))),
         preferred_element_type=F32,
     ).reshape(count * 8, 128)
     coarse = top.astype(BF).astype(F32)
     middle = (top - coarse).astype(BF).astype(F32)
     fine = top - coarse - middle
-    rows = jnp.where(lane < 16, middle, jnp.where(lane < 32, fine, jnp.where(lane < 64, total, out)))
+    rows = jnp.where(lane < 16, middle, jnp.where(lane < 32, fine, out))
     rows = jnp.where(lane < 8, coarse, rows)
     return rows.astype(BF)
 
@@ -100,7 +99,7 @@
     both_o,
     hid_v, again_v, wq_v, wkv_v, wo_v, cache_v, ptab_v, ctx_v, mdest_v, fgain_v, router_v,
     routes_v, win_v, wdown_v, win_f, wgu_v, fold_v, a1_v, qg_v, loc_v,
-    xg, msg, inq, ret_s, ret, rs_s, rs, fg, es_s, es,
+    values_v, xg, msg, inq, ret_s, ret, rs_s, rs, fg, es_s, es,
     isem, ready, ssem, rsem,
 ):
     r = lax.axis_index("replica")
@@ -326,8 +325,11 @@
     exchange(msg, inq, 1)
 
     get_cache.wait()
+    key_lane = iota((8, PAGE, 128), 2) < HEAD_DIM
+    for c in range(0, POOL, 8):
+        values_v[c : c + 8] = jnp.where(key_lane, 1.0, cache_v[c : c + 8].astype(F32)).astype(BF)
     loc_v[0 : LOCAL * 8, :] = page_rows(
-        mm(a1_v[0 : LOCAL * 8, :], qg_v[...]), cache_v[0:LOCAL]
+        mm(a1_v[0 : LOCAL * 8, :], qg_v[...]), cache_v[0:LOCAL], values_v[0:LOCAL]
     )
     if NL > LOCAL * 8:
         loc_v[LOCAL * 8 :, :] = jnp.zeros((NL - LOCAL * 8, 128), BF)
@@ -352,7 +354,7 @@
 
     arrived(inq, rsem, 1)
     sent = inq[...].astype(F32).reshape(NIN, 128).astype(BF)
-    lent = page_rows(mm(fetch, sent), cache_v[LOCAL:POOL])
+    lent = page_rows(mm(fetch, sent), cache_v[LOCAL:POOL], values_v[LOCAL:POOL])
     ret_s[...] = mm(place, lent).reshape(R, ROWS, 128).astype(BF)
     exchange(ret_s, ret, 2)
 
@@ -487,6 +489,7 @@
         vm((NL + NIN, 4 * B), BF),
         vm((4 * B, 128), BF),
         vm((NL, 128), BF),
+        vm((POOL, PAGE, 128), BF),
         group,
         inbox,
         inbox,

time: 48.9 us -> 48.9 us (level)
  no operation moved by 1% of the time
where the time goes in v6:
time: 48.9 us; the launch traced here: 48.6 us
  Pallas kernels  47.4 us (97%)
  between operations  0.64 us (1%)
  local copies, waits for them, and re-layouts  0.61 us (1%)
    pallas_call x1, Pallas kernels, on_device(): pl.pallas_call(functools.partial(kernel, R, T, B, NL, LOCAL, POOL, OUT, U...  47.4 us

profile of v6, /device:TPU:1, one launch (start us, length us, event | category | flops | bytes accessed | tf_op | source)
XLA Modules:
  0.0 48.6 jit_solution(7391447260781533567)
XLA Ops:
  0.6 47.4 %decode_step.1 = bf16[4,3072]{1,0:T(4,128)(2,1)S(1)} custom-call(bf16[4,1536]{1,0:T(4,128)(2,1)} %hid.1, f32[1536]{0:T(1024)} %again.1, bf16[192,1536]{1,0:T(8,128)(2,1)} %bitcast.11, bf16[1536,128]{1,0:T(8,128)(2,1)} %bitcast.12, bf16[192,1536]{1,0:T(8,128)(2,1)} %wo.1, bf16[72,128,128]{2,1,0:T(8,128)(2,1)} %bitcast.9, s32[16,32]{1,0:T(8,128)} %bitcast.14, ...), custom_call_target="tpu_custom_call" | custom-call | tf_op jit(solution)/shard_map/decode_step/pallas_call | solution.py:508
  48.0 0.6 %fusion = (bf16[4,1536]{1,0:T(4,128)(2,1)}, bf16[4,1536]{1,0:T(4,128)(2,1)}) fusion(bf16[4,3072]{1,0:T(4,128)(2,1)S(1)} %decode_step.1), kind=kLoop, calls=%fused_computation | loop fusion | bytes 49152 | tf_op jit(solution)/shard_map/slice | solution.py:519
